TPU v7x, 32 devices: a whole 2x2x4 slice. The times are simulated.
32 devices in a mesh: dp: 8 (over z, y), mp: 4 (over x, core).
Axes of the slice: x: 2, y: 2, z: 4, core: 2. Of those that a mesh axis runs over, the one named last changes fastest.
Arguments:
- token_ids: int32 [16384], P('dp'), may hold values from 0 to 8191
- seg_ids: int32 [16384], P('dp'), may hold values from 0 to 255, as said below
- timesteps: int32 [16384], P('dp'), may hold values from 0 to 1999
- noise: float32 [16384, 128], P('dp'), may hold values from -6 to 6
- table: bfloat16 [8192, 128], P('dp'), may hold values from -6 to 6
- w_in: bfloat16 [128, 768], replicated, may hold values from -0.5 to 0.5
- b_in: float32 [768], replicated, may hold values from -3 to 3
- w_time: bfloat16 [128, 768], replicated, may hold values from -0.5 to 0.5
- gain1: float32 [768], replicated, may hold values from 0.5 to 1.5
- shift1: float32 [768], replicated, may hold values from -2 to 2
- w_qkv: bfloat16 [3, 768, 768], P(None, None, 'mp'), may hold values from -0.21875 to 0.21875
- w_out: bfloat16 [768, 768], P('mp'), may hold values from -3.5 to 3.5
- gain2: float32 [768], replicated, may hold values from 0.5 to 1.5
- shift2: float32 [768], replicated, may hold values from -2 to 2
- w_up: bfloat16 [768, 3072], P(None, 'mp'), may hold values from -0.21875 to 0.21875
- b_up: float32 [3072], P('mp'), may hold values from -2 to 2
- w_down: bfloat16 [3072, 768], P('mp'), may hold values from -0.109375 to 0.109375
- b_down: float32 [768], replicated, may hold values from -2 to 2
- cotangent: float32 [16384, 768], P('dp'), may hold values from -6 to 6
Outputs:
- output: float32 [16384, 768], P('dp')
- grad_table: float32 [8192, 128], P('dp')
- grad_w_in: float32 [128, 768], replicated
- grad_b_in: float32 [768], replicated
- grad_w_time: float32 [128, 768], replicated
- grad_gain1: float32 [768], replicated
- grad_shift1: float32 [768], replicated
- grad_w_qkv: float32 [3, 768, 768], P(None, None, 'mp')
- grad_w_out: float32 [768, 768], P('mp')
- grad_gain2: float32 [768], replicated
- grad_shift2: float32 [768], replicated
- grad_w_up: float32 [768, 3072], P(None, 'mp')
- grad_b_up: float32 [3072], P('mp')
- grad_w_down: float32 [3072, 768], P('mp')
- grad_b_down: float32 [768], replicated
Inputs may be any that keep to these rules, and one draw needn't show every extreme that they name: `seg_ids`: slots fall into aligned runs of 1024; each run is either one document or 16 documents of 64 slots; ids never fall along the slots and differ between runs; the first run is one document and the last is split.
All inputs are finite; a program needn't handle non-finite values.
Results may differ from a plain program's by a relative error of at most 0.017.
Values may be sent and summed in bfloat16 or wider, within the bound.
No kernel may reach another device: no remote copies, remote signals or barrier semaphores. Data moves between devices by JAX's collectives and lax.ppermute only.
A program may use at most 192 MiB of HBM per device.

v0:
```python
import math
import jax
import jax.numpy as jnp
from jax import lax
from jax.sharding import PartitionSpec as P

HD = 64
TSTEPS = 2000
QBLK = 512
NEG_BIG = -1000000000.0


def layer_norm(inputs, gain_vec, shift_vec):
    row_mean = jnp.mean(inputs, axis=-1, keepdims=True)
    centred = inputs - row_mean
    variance = jnp.mean(centred * centred, axis=-1, keepdims=True)
    return centred * lax.rsqrt(variance + 1e-05) * gain_vec + shift_vec


def noise_rates(time_ids, horizon):
    fraction = time_ids.astype(jnp.float32) / horizon
    signal = 1.0 - jnp.sqrt(fraction + 0.0001)
    return (jnp.sqrt(signal), jnp.sqrt(1.0 - signal))


def time_features(time_ids, feat_width):
    half_width = feat_width // 2
    freq_table = jnp.exp(
        -math.log(10000.0) * jnp.arange(half_width, dtype=jnp.float32) / half_width
    )
    angles = time_ids.astype(jnp.float32)[:, None] * freq_table[None, :]
    return jnp.concatenate([jnp.sin(angles), jnp.cos(angles)], axis=1)


def gelu_exact(inputs):
    return jax.nn.gelu(inputs, approximate=False)


def block_rows(array_in, index, block_len):
    return lax.dynamic_slice_in_dim(array_in, index * block_len, block_len, 0)


def masked_scores(query_blk, key_blk, seg_query, seg_key):
    scaled = jnp.einsum(
        "qhd,khd->hqk", query_blk, key_blk, preferred_element_type=jnp.float32
    ) * query_blk.shape[-1] ** (-0.5)
    same_seg = seg_query[:, None] == seg_key[None, :]
    return jnp.where(same_seg[None], scaled, NEG_BIG)


def attend_forward(queries, keys_all, values_all, seg_ids, block_len):
    token_count, head_count, head_width = queries.shape
    block_count = token_count // block_len

    def query_block(q_index):
        query_blk = block_rows(queries, q_index, block_len)
        seg_query = block_rows(seg_ids, q_index, block_len)

        def stats_step(k_index, current):
            row_top, row_sum = current
            scores = masked_scores(
                query_blk,
                block_rows(keys_all, k_index, block_len),
                seg_query,
                block_rows(seg_ids, k_index, block_len),
            )
            new_top = jnp.maximum(row_top, jnp.max(scores, axis=-1))
            new_sum = row_sum * jnp.exp(row_top - new_top) + jnp.sum(
                jnp.exp(scores - new_top[:, :, None]), axis=-1
            )
            return (new_top, new_sum)

        start_stats = (
            jnp.full((head_count, block_len), NEG_BIG, jnp.float32),
            jnp.zeros((head_count, block_len), jnp.float32),
        )
        row_top, row_sum = lax.fori_loop(0, block_count, stats_step, start_stats)

        def value_step(k_index, current):
            scores = masked_scores(
                query_blk,
                block_rows(keys_all, k_index, block_len),
                seg_query,
                block_rows(seg_ids, k_index, block_len),
            )
            weights_bf = (jnp.exp(scores - row_top[:, :, None]) / row_sum[:, :, None]).astype(
                jnp.bfloat16
            )
            return current + jnp.einsum(
                "hqk,khd->qhd",
                weights_bf,
                block_rows(values_all, k_index, block_len),
                preferred_element_type=jnp.float32,
            )

        mixed_blk = lax.fori_loop(
            0, block_count, value_step, jnp.zeros((block_len, head_count, head_width), jnp.float32)
        )
        return (mixed_blk, row_top, row_sum)

    mixed_all, tops, sums = lax.map(query_block, jnp.arange(block_count))
    return (mixed_all.reshape(token_count, head_count, head_width), tops, sums)


def attend_backward(queries, keys_all, values_all, grad_mixed, seg_ids, tops, sums, block_len):
    token_count, head_count, head_width = queries.shape
    block_count = token_count // block_len
    scale_factor = head_width ** (-0.5)

    def query_step(q_index, totals):
        grad_q_all, grad_k_all, grad_v_all = totals
        query_blk = block_rows(queries, q_index, block_len)
        grad_blk = block_rows(grad_mixed, q_index, block_len)
        seg_query = block_rows(seg_ids, q_index, block_len)
        row_top = tops[q_index]
        row_sum = sums[q_index]

        def probs_for(k_index):
            key_blk = block_rows(keys_all, k_index, block_len)
            value_blk = block_rows(values_all, k_index, block_len)
            scores = masked_scores(
                query_blk, key_blk, seg_query, block_rows(seg_ids, k_index, block_len)
            )
            weights = jnp.exp(scores - row_top[:, :, None]) / row_sum[:, :, None]
            grad_weights = jnp.einsum(
                "qhd,khd->hqk", grad_blk, value_blk, preferred_element_type=jnp.float32
            )
            return (key_blk, weights, grad_weights)

        def delta_step(k_index, current):
            key_blk, weights, grad_weights = probs_for(k_index)
            return current + jnp.sum(grad_weights * weights, axis=-1)

        delta = lax.fori_loop(
            0, block_count, delta_step, jnp.zeros((head_count, block_len), jnp.float32)
        )

        def grad_step(k_index, current):
            grad_query, grad_keys, grad_values = current
            key_blk, weights, grad_weights = probs_for(k_index)
            grad_scores = (weights * (grad_weights - delta[:, :, None])).astype(jnp.bfloat16)
            grad_query = (
                grad_query
                + jnp.einsum(
                    "hqk,khd->qhd", grad_scores, key_blk, preferred_element_type=jnp.float32
                )
                * scale_factor
            )
            key_part = (
                jnp.einsum(
                    "hqk,qhd->khd", grad_scores, query_blk, preferred_element_type=jnp.float32
                )
                * scale_factor
            )
            value_part = jnp.einsum(
                "hqk,qhd->khd",
                weights.astype(jnp.bfloat16),
                grad_blk,
                preferred_element_type=jnp.float32,
            )
            grad_keys = lax.dynamic_update_slice_in_dim(
                grad_keys,
                block_rows(grad_keys, k_index, block_len) + key_part,
                k_index * block_len,
                0,
            )
            grad_values = lax.dynamic_update_slice_in_dim(
                grad_values,
                block_rows(grad_values, k_index, block_len) + value_part,
                k_index * block_len,
                0,
            )
            return (grad_query, grad_keys, grad_values)

        start_grads = (
            jnp.zeros((block_len, head_count, head_width), jnp.float32),
            grad_k_all,
            grad_v_all,
        )
        grad_query, grad_k_all, grad_v_all = lax.fori_loop(0, block_count, grad_step, start_grads)
        grad_q_all = lax.dynamic_update_slice_in_dim(grad_q_all, grad_query, q_index * block_len, 0)
        return (grad_q_all, grad_k_all, grad_v_all)

    zeros_all = jnp.zeros(queries.shape, jnp.float32)
    return lax.fori_loop(0, block_count, query_step, (zeros_all, zeros_all, zeros_all))


def body(
    token_ids,
    seg_ids,
    timesteps,
    noise,
    table,
    w_in,
    b_in,
    w_time,
    gain1,
    shift1,
    w_qkv,
    w_out,
    gain2,
    shift2,
    w_up,
    b_up,
    w_down,
    b_down,
    cotangent,
):
    whole_table = lax.all_gather(table, "dp", axis=0, tiled=True)
    table_full = whole_table.astype(jnp.float32)
    vocab_rows, embed_width = table_full.shape
    row_norms = jnp.sqrt(jnp.sum(table_full * table_full, axis=1) + 1e-06)
    mean_norm = jnp.mean(row_norms)
    factor = math.sqrt(embed_width) / mean_norm
    looked_up = jnp.take(table_full, token_ids, axis=0)
    clean_rows = looked_up * factor
    keep_rate, noise_rate = noise_rates(timesteps, TSTEPS)
    noisy_in = (keep_rate[:, None] * clean_rows + noise_rate[:, None] * noise).astype(jnp.bfloat16)
    features = time_features(timesteps, w_time.shape[0]).astype(jnp.bfloat16)
    hidden = (
        jnp.dot(noisy_in, w_in, preferred_element_type=jnp.float32)
        + jnp.dot(features, w_time, preferred_element_type=jnp.float32)
        + b_in
    )
    token_count = hidden.shape[0]
    act_one_f, norm_one_back = jax.vjp(layer_norm, hidden, gain1, shift1)
    act_one = act_one_f.astype(jnp.bfloat16)
    projected = jnp.einsum(
        "td,cdk->ctk", act_one, w_qkv, preferred_element_type=jnp.float32
    ).astype(jnp.bfloat16)
    head_count = w_qkv.shape[2] // HD
    heads_all = projected.reshape(3, token_count, head_count, HD)
    queries, keys_all, values_all = (heads_all[0], heads_all[1], heads_all[2])
    mixed_f, tops, sums = attend_forward(queries, keys_all, values_all, seg_ids, QBLK)
    mixed = mixed_f.astype(jnp.bfloat16).reshape(token_count, head_count * HD)
    attn_part = jnp.dot(mixed, w_out, preferred_element_type=jnp.float32)
    resid = hidden + lax.psum(attn_part, "mp")
    act_two_f, norm_two_back = jax.vjp(layer_norm, resid, gain2, shift2)
    act_two = act_two_f.astype(jnp.bfloat16)
    pre_act = jnp.dot(act_two, w_up, preferred_element_type=jnp.float32) + b_up
    activated_f, gelu_back = jax.vjp(gelu_exact, pre_act)
    activated = activated_f.astype(jnp.bfloat16)
    down_part = jnp.dot(activated, w_down, preferred_element_type=jnp.float32)
    output = resid + lax.psum(down_part.astype(jnp.bfloat16), "mp").astype(jnp.float32) + b_down
    cot_rounded = cotangent.astype(jnp.bfloat16)
    grad_w_down = jnp.einsum(
        "tf,td->fd", activated, cot_rounded, preferred_element_type=jnp.float32
    )
    grad_b_down = jnp.sum(cotangent, axis=0)
    grad_gelu = jnp.einsum("td,fd->tf", cot_rounded, w_down, preferred_element_type=jnp.float32)
    (grad_pre,) = gelu_back(grad_gelu)
    grad_pre_r = grad_pre.astype(jnp.bfloat16)
    grad_w_up = jnp.einsum("td,tf->df", act_two, grad_pre_r, preferred_element_type=jnp.float32)
    grad_b_up = jnp.sum(grad_pre_r.astype(jnp.float32), axis=0)
    grad_two_part = jnp.einsum("tf,df->td", grad_pre_r, w_up, preferred_element_type=jnp.float32)
    grad_act_two = lax.psum(grad_two_part, "mp")
    grad_resid_norm, grad_gain2, grad_shift2 = norm_two_back(grad_act_two)
    grad_resid = cotangent + grad_resid_norm
    grad_attn_r = grad_resid.astype(jnp.bfloat16)
    grad_w_out = jnp.einsum("tk,td->kd", mixed, grad_attn_r, preferred_element_type=jnp.float32)
    grad_mixed = (
        jnp.einsum("td,kd->tk", grad_attn_r, w_out, preferred_element_type=jnp.float32)
        .astype(jnp.bfloat16)
        .reshape(token_count, head_count, HD)
    )
    grad_q, grad_k, grad_v = attend_backward(
        queries, keys_all, values_all, grad_mixed, seg_ids, tops, sums, QBLK
    )
    grad_proj = jnp.stack(
        [grad_q.astype(jnp.bfloat16), grad_k.astype(jnp.bfloat16), grad_v.astype(jnp.bfloat16)]
    ).reshape(3, token_count, head_count * HD)
    grad_w_qkv = jnp.einsum("td,ctk->cdk", act_one, grad_proj, preferred_element_type=jnp.float32)
    grad_one_part = jnp.einsum("ctk,cdk->td", grad_proj, w_qkv, preferred_element_type=jnp.float32)
    grad_act_one = lax.psum(grad_one_part.astype(jnp.bfloat16), "mp").astype(jnp.float32)
    grad_hidden_norm, grad_gain1, grad_shift1 = norm_one_back(grad_act_one)
    grad_hidden_r = (grad_resid + grad_hidden_norm).astype(jnp.bfloat16)
    grad_w_in = jnp.einsum("te,td->ed", noisy_in, grad_hidden_r, preferred_element_type=jnp.float32)
    grad_w_time = jnp.einsum(
        "te,td->ed", features, grad_hidden_r, preferred_element_type=jnp.float32
    )
    grad_b_in = jnp.sum(grad_hidden_r.astype(jnp.float32), axis=0)
    grad_noisy = jnp.einsum("td,ed->te", grad_hidden_r, w_in, preferred_element_type=jnp.float32)
    grad_clean = keep_rate[:, None] * grad_noisy
    scaled_grad = grad_clean * factor
    norm_coeff = -jnp.sum(grad_clean * looked_up) * factor / (mean_norm * vocab_rows)
    unit_rows = table_full / row_norms[:, None]
    row_count = lax.axis_size("dp") * table.shape[0]
    inside = (token_ids >= 0) & (token_ids < row_count)
    slot_ids = jnp.where(inside, token_ids, row_count)
    direct = jax.ops.segment_sum(scaled_grad, slot_ids, num_segments=row_count + 1)[:row_count]
    grad_table = lax.psum_scatter(
        direct + norm_coeff * unit_rows, "dp", scatter_dimension=0, tiled=True
    )
    summed = tuple(
        lax.psum(
            (
                grad_w_in,
                grad_b_in,
                grad_w_time,
                grad_gain1,
                grad_shift1,
                grad_w_qkv,
                grad_w_out,
                grad_gain2,
                grad_shift2,
                grad_w_up,
                grad_b_up,
                grad_w_down,
                grad_b_down,
            ),
            "dp",
        )
    )
    return (
        output,
        grad_table,
        summed[0],
        summed[1],
        summed[2],
        summed[3],
        summed[4],
        summed[5],
        summed[6],
        summed[7],
        summed[8],
        summed[9],
        summed[10],
        summed[11],
        summed[12],
    )


def solution(mesh):
    in_specs = (
        P("dp"),
        P("dp"),
        P("dp"),
        P("dp", None),
        P("dp", None),
        P(),
        P(),
        P(),
        P(),
        P(),
        P(None, None, "mp"),
        P("mp", None),
        P(),
        P(),
        P(None, "mp"),
        P("mp"),
        P("mp", None),
        P(),
        P("dp", None),
    )
    out_specs = (
        P("dp", None),
        P("dp", None),
        P(),
        P(),
        P(),
        P(),
        P(),
        P(None, None, "mp"),
        P("mp", None),
        P(),
        P(),
        P(None, "mp"),
        P("mp"),
        P("mp", None),
        P(),
    )
    return jax.shard_map(body, mesh=mesh, in_specs=in_specs, out_specs=out_specs, check_vma=False)
```

profile of v0, /device:TPU:0, one launch (start us, length us, event | category | flops | bytes accessed | tf_op | source)
XLA Modules:
  0.0 1170.5 jit_solution(15731865098663500380)
XLA Ops:
  13.5 48.5 %all-gather.2.cloned.1.call-done = bf16[8192,128]{1,0:T(8,128)(2,1)} async-done(((bf16[1024,128]{1,0:T(8,128)(2,1)}), bf16[8192,128]{1,0:T(8,128)(2,1)}) %all-gather.2.cloned.1.call-update) | async-done | bytes 2097168 | tf_op jit(solution)/shard_map/all_gather | solution.py:209
  70.5 7.7 gather_fusion
  90.6 98.2 %while.123 = (s32[]{:T(128)}, bf16[4,512,3,64]{1,3,2,0:T(8,128)(2,1)}, f32[4,3,512]{2,1,0:T(4,128)}, f32[4,3,512]{2,1,0:T(4,128)}, s32[4]{0:T(128)S(1)}, /*index...) while((s32[]{:T(128)}, ...), condition=%wide.region_11.12_spmd, body=%wide.region_4.11_spmd.sunk | while | flops 312155648 | bytes 10699101 | solution.py:101
  92.8 7.4 while.127
  100.9 12.5 %while.128 = (s32[]{:T(128)}, f32[512,3,64]{0,2,1:T(8,128)}, bf16[2048,3,64]{0,2,1:T(8,128)(2,1)S(1)}, s32[512]{0:T(512)S(1)}, s32[2048]{0:T(1024)S(1)}, /*index...) while((s32[]{:T(128)}, f32[512,3,64]{0,2,1:T(8,128)}, ...), condition=%wide.region_10.10_spmd.clone, body=%wide.region_9.9_spmd.clone.sunk | while | flops 205717504 | bytes 1926848 | solution.py:96
  117.3 7.4 while.127
  125.4 12.5 %while.128 = (s32[]{:T(128)}, f32[512,3,64]{0,2,1:T(8,128)}, bf16[2048,3,64]{0,2,1:T(8,128)(2,1)S(1)}, s32[512]{0:T(512)S(1)}, s32[2048]{0:T(1024)S(1)}, /*index...) while((s32[]{:T(128)}, f32[512,3,64]{0,2,1:T(8,128)}, ...), condition=%wide.region_10.10_spmd.clone, body=%wide.region_9.9_spmd.clone.sunk | while | flops 205717504 | bytes 1926848 | solution.py:96
  141.8 7.4 while.127
  149.8 12.5 %while.128 = (s32[]{:T(128)}, f32[512,3,64]{0,2,1:T(8,128)}, bf16[2048,3,64]{0,2,1:T(8,128)(2,1)S(1)}, s32[512]{0:T(512)S(1)}, s32[2048]{0:T(1024)S(1)}, /*index...) while((s32[]{:T(128)}, f32[512,3,64]{0,2,1:T(8,128)}, ...), condition=%wide.region_10.10_spmd.clone, body=%wide.region_9.9_spmd.clone.sunk | while | flops 205717504 | bytes 1926848 | solution.py:96
  166.3 7.4 while.127
  174.3 12.5 %while.128 = (s32[]{:T(128)}, f32[512,3,64]{0,2,1:T(8,128)}, bf16[2048,3,64]{0,2,1:T(8,128)(2,1)S(1)}, s32[512]{0:T(512)S(1)}, s32[2048]{0:T(1024)S(1)}, /*index...) while((s32[]{:T(128)}, f32[512,3,64]{0,2,1:T(8,128)}, ...), condition=%wide.region_10.10_spmd.clone, body=%wide.region_9.9_spmd.clone.sunk | while | flops 205717504 | bytes 1926848 | solution.py:96
  195.6 118.2 %all-reduce.8.cloned.1.call-done = f32[2048,768]{0,1:T(8,128)} async-done(((f32[2048,768]{0,1:T(8,128)}), f32[2048,768]{0,1:T(8,128)}) %all-reduce.8.cloned.1.call-update) | async-done | bytes 6291472 | tf_op jit(solution)/shard_map/psum | solution.py:237
  323.0 18.8 %multiply_convert_fusion = (bf16[2048,768]{1,0:T(8,128)(2,1)}, f32[2048,768]{1,0:T(8,128)}, f32[2048,768]{1,0:T(8,128)}) fusion(f32[768]{0:T(1024)S(1)} %copy-done.63, bf16[2048,768]{0,1:T(8,128)(2,1)S(1)} %add_convert_fusion.2, bf16[768,768]{1,0:T(8,128)(2,1)S(1)} %copy-done), kind=kOutput, calls=%fused_computation.93 | convolution fusion | flops 2519728128 | bytes 20057088 | tf_op jit(solution)/shard_map/dot_general | solution.py:240
  341.8 8.1 convert_reduce_fusion.1
  356.1 7.0 copy.74
  370.1 105.9 %all-reduce.10.cloned.1.call-done = f32[2048,768]{0,1:T(8,128)} async-done(((f32[2048,768]{0,1:T(8,128)}), f32[2048,768]{0,1:T(8,128)}) %all-reduce.10.cloned.1.call-update) | async-done | bytes 6291472 | tf_op jit(solution)/shard_map/psum | solution.py:256
  492.9 161.6 %while.126 = (s32[]{:T(128)}, bf16[2048,3,64]{0,2,1:T(8,128)(2,1)}, f32[2048,3,64]{0,2,1:T(8,128)}, f32[2048,3,64]{0,2,1:T(8,128)S(1)}, bf16[2048,3,64]{0,2,1:T(...) while((s32[]{:T(128)}, bf16[2048,3,64]{0,2,1:T(8,128)(2,1)}, ...), condition=%wide.region_25.26_spmd, body=%wide.region_19.25_spmd.sunk | while | flops 716768768 | bytes 27696096 | solution.py:185
  494.7 12.6 %while.129 = (s32[]{:T(128)}, f32[3,512]{1,0:T(4,128)S(1)}, bf16[2048,3,64]{0,2,1:T(8,128)(2,1)}, bf16[512,3,64]{0,2,1:T(8,128)(2,1)S(1)}, s32[512]{0:T(512)S(1)...) while((s32[]{:T(128)}, f32[3,512]{1,0:T(4,128)S(1)}, ...), condition=%wide.region_22.22_spmd.clone, body=%wide.region_20.21_spmd.clone.sunk | while | flops 206308864 | bytes 7647441 | solution.py:134
  507.3 25.2 %while.130 = (s32[]{:T(128)}, f32[512,3,64]{0,2,1:T(8,128)S(1)}, f32[2048,3,64]{0,2,1:T(8,128)}, f32[2048,3,64]{0,2,1:T(8,128)S(1)}, bf16[2048,3,64]{0,2,1:T(8,1...) while((s32[]{:T(128)}, f32[512,3,64]{0,2,1:T(8,128)S(1)}, ...), condition=%wide.region_24.24_spmd.clone, body=%wide.region_23.23_spmd.clone.sunk | while | flops 510459904 | bytes 18446580 | solution.py:180
  535.1 12.6 %while.129 = (s32[]{:T(128)}, f32[3,512]{1,0:T(4,128)S(1)}, bf16[2048,3,64]{0,2,1:T(8,128)(2,1)}, bf16[512,3,64]{0,2,1:T(8,128)(2,1)S(1)}, s32[512]{0:T(512)S(1)...) while((s32[]{:T(128)}, f32[3,512]{1,0:T(4,128)S(1)}, ...), condition=%wide.region_22.22_spmd.clone, body=%wide.region_20.21_spmd.clone.sunk | while | flops 206308864 | bytes 7647441 | solution.py:134
  547.7 25.2 %while.130 = (s32[]{:T(128)}, f32[512,3,64]{0,2,1:T(8,128)S(1)}, f32[2048,3,64]{0,2,1:T(8,128)}, f32[2048,3,64]{0,2,1:T(8,128)S(1)}, bf16[2048,3,64]{0,2,1:T(8,1...) while((s32[]{:T(128)}, f32[512,3,64]{0,2,1:T(8,128)S(1)}, ...), condition=%wide.region_24.24_spmd.clone, body=%wide.region_23.23_spmd.clone.sunk | while | flops 510459904 | bytes 18446580 | solution.py:180
  575.5 12.6 %while.129 = (s32[]{:T(128)}, f32[3,512]{1,0:T(4,128)S(1)}, bf16[2048,3,64]{0,2,1:T(8,128)(2,1)}, bf16[512,3,64]{0,2,1:T(8,128)(2,1)S(1)}, s32[512]{0:T(512)S(1)...) while((s32[]{:T(128)}, f32[3,512]{1,0:T(4,128)S(1)}, ...), condition=%wide.region_22.22_spmd.clone, body=%wide.region_20.21_spmd.clone.sunk | while | flops 206308864 | bytes 7647441 | solution.py:134
  588.1 25.2 %while.130 = (s32[]{:T(128)}, f32[512,3,64]{0,2,1:T(8,128)S(1)}, f32[2048,3,64]{0,2,1:T(8,128)}, f32[2048,3,64]{0,2,1:T(8,128)S(1)}, bf16[2048,3,64]{0,2,1:T(8,1...) while((s32[]{:T(128)}, f32[512,3,64]{0,2,1:T(8,128)S(1)}, ...), condition=%wide.region_24.24_spmd.clone, body=%wide.region_23.23_spmd.clone.sunk | while | flops 510459904 | bytes 18446580 | solution.py:180
  615.9 12.6 %while.129 = (s32[]{:T(128)}, f32[3,512]{1,0:T(4,128)S(1)}, bf16[2048,3,64]{0,2,1:T(8,128)(2,1)}, bf16[512,3,64]{0,2,1:T(8,128)(2,1)S(1)}, s32[512]{0:T(512)S(1)...) while((s32[]{:T(128)}, f32[3,512]{1,0:T(4,128)S(1)}, ...), condition=%wide.region_22.22_spmd.clone, body=%wide.region_20.21_spmd.clone.sunk | while | flops 206308864 | bytes 7647441 | solution.py:134
  628.4 25.2 %while.130 = (s32[]{:T(128)}, f32[512,3,64]{0,2,1:T(8,128)S(1)}, f32[2048,3,64]{0,2,1:T(8,128)}, f32[2048,3,64]{0,2,1:T(8,128)S(1)}, bf16[2048,3,64]{0,2,1:T(8,1...) while((s32[]{:T(128)}, f32[512,3,64]{0,2,1:T(8,128)S(1)}, ...), condition=%wide.region_24.24_spmd.clone, body=%wide.region_23.23_spmd.clone.sunk | while | flops 510459904 | bytes 18446580 | solution.py:180
  670.3 7.1 fusion.70
  682.7 100.5 %all-reduce.14.cloned.1.call-done = (bf16[2048,768]{0,1:T(8,128)(2,1)}, bf16[2048,768]{0,1:T(8,128)(2,1)}) async-done(((bf16[2048,768]{0,1:T(8,128)(2,1)}, bf16[2048,768]{0,1:T(8,128)(2,1)}), (bf16[2048,768]{0,1:T(8,128)(2,1)}, bf16[2048,768]{0,1:T(8,128)(2,1)})) %all-reduce.14.cloned.1.call-update) | async-done | bytes 6291472 | tf_op jit(solution)/shard_map/psum | solution.py:244
  811.0 13.1 %scatter_custom_fusion = f32[8193,128]{1,0:T(8,128)} fusion(s32[2048]{0:T(1024)} %get-tuple-element.1347, f32[]{:T(128)} %constant.325.clone.1, f32[2048,128]{1,0:T(8,128)} %get-tuple-element.1355, f32[]{:T(128)S(6)} %div.136), kind=kCustom, calls=%fused_computation.122 | custom fusion | flops 524288 | bytes 5243908 | tf_op jit(solution)/shard_map/scatter-add | solution.py:290
  834.0 7.1 add_add_fusion.3
  847.8 40.1 %all-reduce = (f32[768]{0:T(1024)}, f32[768]{0:T(1024)}, f32[768]{0:T(1024)}, f32[768]{0:T(1024)}, f32[768]{0:T(1024)}, /*index=5*/f32[768]{0:T(1024)}, f32[768]{0:T(1024)}) all-reduce(f32[768]{0:T(1024)S(1)} %get-tuple-element.1324, f32[768]{0:T(1024)S(1)} %get-tuple-element.1186, ...), channel_id=1, replica_groups=mesh['dp'=8,'mp'=4] {'dp'}, use_global_device_ids=true, to_apply=%region_34.35 | all-reduce | flops 5376 | bytes 43008 | tf_op jit(solution)/shard_map/psum | solution.py:295
  887.9 172.8 %all-reduce.12.cloned.1.call-done = (f32[128,768]{1,0:T(8,128)}, f32[128,768]{1,0:T(8,128)}, f32[3,768,192]{1,2,0:T(8,128)}, f32[192,768]{1,0:T(8,128)}, f32[768,768]{1,0:T(8,128)}, /*index=5*/f32[768,768]{1,0:T(8,128)}) async-done(((f32[128,768]{1,0:T(8,128)}, f32[128,768]{1,0:T(8,128)}, f32[3,768,192]{1,2,0:T(8,128)}, f32[192,768]{1,0:T(8,128)}, f32[768,768]{1,0:T(8,128)}, ...) | async-done | bytes 7864336 | tf_op jit(solution)/shard_map/psum | solution.py:295
  1060.6 91.4 %reduce-scatter.2.cloned.1.call-done = f32[1024,128]{1,0:T(8,128)} async-done(((f32[8192,128]{1,0:T(8,128)}), f32[1024,128]{1,0:T(8,128)}) %reduce-scatter.2.cloned.1.call-update) | async-done | bytes 524304 | tf_op jit(solution)/shard_map/reduce_scatter | solution.py:291
  (635 shorter events, 401.3 us)
Async XLA Ops:
  7.2 315.8 %copy-start = (bf16[768,768]{1,0:T(8,128)(2,1)S(1)}, bf16[768,768]{1,0:T(8,128)(2,1)}, u32[]{:S(2)}) copy-start(bf16[768,768]{1,0:T(8,128)(2,1)} %param.45) | copy-start | bytes 3538948
  7.2 54.8 %all-gather.2.cloned.1.call-start = ((), (), s32[]{:S(2)}) async-start(), calls=%async_computation.1 | async-start | bytes 2359296 | tf_op jit(solution)/shard_map/all_gather | solution.py:209
  7.9 305.9 %all-reduce.8.cloned.1.call-start = ((), (), s32[]{:S(2)}) async-start(), calls=%async_computation.2 | async-start | bytes 12582912 | tf_op jit(solution)/shard_map/psum | solution.py:237
  9.4 68.8 %copy-start.51 = (pred[2048]{0:T(1024)(128)(4,1)}, pred[2048]{0:T(1024)(128)(4,1)S(1)}, u32[]{:S(2)}) copy-start(pred[2048]{0:T(1024)(128)(4,1)S(1)} %compare_and_fusion) | copy-start | bytes 6148
  11.4 66.8 %copy-start.39 = (f32[2048]{0:T(1024)}, f32[2048]{0:T(1024)S(1)}, u32[]{:S(2)}) copy-start(f32[2048]{0:T(1024)S(1)} %get-tuple-element.1349) | copy-start | bytes 24580
  13.5 69.2 %copy-start.23 = (bf16[2048,64]{0,1:T(8,128)(2,1)}, bf16[2048,64]{0,1:T(8,128)(2,1)S(1)}, u32[]{:S(2)}) copy-start(bf16[2048,64]{0,1:T(8,128)(2,1)S(1)} %get-tuple-element.1345) | copy-start | bytes 786436
  13.5 69.2 %copy-start.25 = (bf16[2048,64]{0,1:T(8,128)(2,1)}, bf16[2048,64]{0,1:T(8,128)(2,1)S(1)}, u32[]{:S(2)}) copy-start(bf16[2048,64]{0,1:T(8,128)(2,1)S(1)} %get-tuple-element.1346) | copy-start | bytes 786436
  70.5 11.1 copy-start.35
  90.5 101.3 %copy-start.29 = (bf16[192,768]{1,0:T(8,128)(2,1)S(1)}, bf16[192,768]{1,0:T(8,128)(2,1)}, u32[]{:S(2)}) copy-start(bf16[192,768]{1,0:T(8,128)(2,1)} %param.42) | copy-start | bytes 884740
  195.6 280.5 %all-reduce.10.cloned.1.call-start = ((), (), s32[]{:S(2)}) async-start(), calls=%async_computation.3 | async-start | bytes 12582912 | tf_op jit(solution)/shard_map/psum | solution.py:256
  320.8 20.9 %slice-start.2 = ((s8[6291456]{0:T(1024)(128)(4,1)}), s8[4194304]{0:T(1024)(128)(4,1)S(1)}, s32[]{:S(2)}) async-start(s8[6291456]{0:T(1024)(128)(4,1)} %bitcast.204), calls=%async_computation.9 | async-start | bytes 8388608
  322.9 18.8 %copy-start.21 = (bf16[2048,768]{0,1:T(8,128)(2,1)}, bf16[2048,768]{0,1:T(8,128)(2,1)S(1)}, u32[]{:S(2)}) copy-start(bf16[2048,768]{0,1:T(8,128)(2,1)S(1)} %add_convert_fusion.2) | copy-start | bytes 9437188
  322.9 18.8 %slice-start.3 = ((s8[6291456]{0:T(1024)(128)(4,1)}), s8[2097152]{0:T(1024)(128)(4,1)S(1)}, s32[]{:S(2)}) async-start(s8[6291456]{0:T(1024)(128)(4,1)} %bitcast.204), calls=%async_computation.10 | async-start | bytes 4194304
  322.9 18.8 %copy-start.61 = (bf16[768,768]{1,0:T(8,128)(2,1)S(1)}, bf16[768,768]{1,0:T(8,128)(2,1)}, u32[]{:S(2)}) copy-start(bf16[768,768]{1,0:T(8,128)(2,1)} %param.47) | copy-start | bytes 3538948
  356.1 427.0 %all-reduce.14.cloned.1.call-start = ((), (), s32[]{:S(2)}) async-start(), calls=%async_computation.6 | async-start | bytes 12582912 | tf_op jit(solution)/shard_map/psum | solution.py:244
  476.0 10.6 slice-start.4
  663.2 397.5 %all-reduce.12.cloned.1.call-start = ((), (), s32[]{:S(2)}) async-start(), calls=%async_computation.5 | async-start | bytes 15728640 | tf_op jit(solution)/shard_map/psum | solution.py:295
  670.2 9.1 copy-start.20
  670.2 9.1 copy-start.30
  670.2 9.1 copy-start.32
  679.4 103.8 %copy-start.38 = (f32[2048]{0:T(1024)S(1)}, f32[2048]{0:T(1024)}, u32[]{:S(2)}) copy-start(f32[2048]{0:T(1024)} %copy-done.37) | copy-start | bytes 24580
  679.4 103.7 %copy-start.50 = (f32[768]{0:T(1024)S(1)}, f32[768]{0:T(1024)}, u32[]{:S(2)}) copy-start(f32[768]{0:T(1024)} %param.39) | copy-start | bytes 9220
  679.4 115.2 %slice-start.6 = ((s8[6291456]{0:T(1024)(128)(4,1)}), s8[2097152]{0:T(1024)(128)(4,1)S(1)}, s32[]{:S(2)}) async-start(s8[6291456]{0:T(1024)(128)(4,1)} %bitcast.208), calls=%async_computation.13 | async-start | bytes 4194304
  682.7 106.2 %copy-start.48 = (f32[2048]{0:T(1024)S(1)}, f32[2048]{0:T(1024)}, u32[]{:S(2)}) copy-start(f32[2048]{0:T(1024)} %copy-done.47) | copy-start | bytes 24580
  682.7 106.3 %copy-start.44 = (f32[2048]{0:T(1024)S(1)}, f32[2048]{0:T(1024)}, u32[]{:S(2)}) copy-start(f32[2048]{0:T(1024)} %copy-done.43) | copy-start | bytes 24580
  783.1 11.5 slice-start
  783.1 11.5 slice-start.7
  804.5 19.6 %copy-start.11 = (bf16[8192,128]{1,0:T(8,128)(2,1)S(1)}, bf16[8192,128]{1,0:T(8,128)(2,1)}, u32[]{:S(2)}) copy-start(bf16[8192,128]{1,0:T(8,128)(2,1)} %all-gather.2.cloned.1.call-done) | copy-start | bytes 6291460
  804.5 19.6 %copy-start.42 = (f32[8192]{0:T(1024)S(1)}, f32[8192]{0:T(1024)}, u32[]{:S(2)}) copy-start(f32[8192]{0:T(1024)} %get-tuple-element.1343) | copy-start | bytes 98308
  804.5 347.5 %reduce-scatter.2.cloned.1.call-start = ((), (), s32[]{:S(2)}) async-start(), calls=%async_computation.4 | async-start | bytes 4718592 | tf_op jit(solution)/shard_map/reduce_scatter | solution.py:291
  1060.6 101.3 %copy-start.27 = (f32[768,768]{1,0:T(8,128)S(1)}, f32[768,768]{1,0:T(8,128)}, u32[]{:S(2)}) copy-start(f32[768,768]{1,0:T(8,128)} %get-tuple-element.2138) | copy-start | bytes 7077892
  1153.9 9.4 copy-start.1
  (47 other events, 178.9 us)
Sparse Core Ops, SparseCore 0:
  10.1 51.7 all-gather.1
  195.7 118.1 all-reduce.7
  356.2 119.7 all-reduce.9
  663.3 119.7 all-reduce.13
  804.6 256.0 all-reduce.11
  1064.7 87.2 reduce-scatter.1
where the time goes:
time: 1180 us; the launch traced here: 1170 us
  waiting for transfers between devices  638 us (54%)
  matrix products  279 us (24%)
  other arithmetic  115 us (10%)
  local copies, waits for them, and re-layouts  75.5 us (6%)
  blocking collectives  40.1 us (3%)
  between operations  17.5 us (1%)
    psum x1, waiting for transfers between devices, body(): lax.psum((grad_w_in, grad_b_in, grad_w_time, grad_gain1, grad_shift1, gra...  173 us
    psum x1, waiting for transfers between devices, body(): resid = hidden + lax.psum(attn_part, 'mp')  118 us
    psum x1, waiting for transfers between devices, body(): grad_act_two = lax.psum(grad_two_part, 'mp')  106 us
    psum x1, waiting for transfers between devices, body(): lax.psum(down_part.astype(jnp.bfloat16), 'mp').astype(jnp.float32)  100 us
    reduce_scatter x1, waiting for transfers between devices, body(): lax.psum_scatter(direct + norm_coeff * unit_rows, 'dp', scatter_dimension...  91.4 us
    dot_general x32, matrix products, probs_for(): jnp.einsum('qhd,khd->hqk', grad_blk, value_blk, preferred_element_type=jn...  59.4 us
    all_gather x1, waiting for transfers between devices, body(): whole_table = lax.all_gather(table, 'dp', axis=0, tiled=True)  48.5 us
    dot_general x16, matrix products, value_step(): jnp.einsum('hqk,khd->qhd', weights_bf, block_rows(values_all, k_index, bl...  45.2 us
  transfers between devices with their start and end apart: 6, of which 6 were waited for; matrix products, arithmetic and copies ran while one was open for 7% of the time, Pallas kernels for 0%

commit v1 on v0

--- a/solution.py
+++ b/solution.py
@@ -206,7 +206,14 @@
     b_down,
     cotangent,
 ):
-    whole_table = lax.all_gather(table, "dp", axis=0, tiled=True)
+    value = table
+    ways, here, step = (lax.axis_size("dp"), lax.axis_index("dp"), value.shape[0])
+    dims = [n * ways if d == 0 else n for d, n in enumerate(value.shape)]
+    full = lax.dynamic_update_slice_in_dim(jnp.zeros(dims, value.dtype), value, here * step, axis=0)
+    for far in range(1, ways):
+        value = lax.ppermute(value, "dp", [(d, (d + 1) % ways) for d in range(ways)])
+        full = lax.dynamic_update_slice_in_dim(full, value, (here - far) % ways * step, axis=0)
+    whole_table = full
     table_full = whole_table.astype(jnp.float32)
     vocab_rows, embed_width = table_full.shape
     row_norms = jnp.sqrt(jnp.sum(table_full * table_full, axis=1) + 1e-06)

time: 1180 us -> 1190 us (level)
    ppermute x0 -> x7, waiting for transfers between devices: none -> 52.7 us  [body(): lax.ppermute(value, 'dp', [(d, (d + 1) % ways) for d in range(ways)])]
    all_gather x1 -> x0, waiting for transfers between devices: 48.5 us -> none  [body(): whole_table = lax.all_gather(table, 'dp', axis=0, tiled=True)]
    unnamed x155 -> x165, local copies, waits for them, and re-layouts: 32.4 us -> 32.7 us
  transfers between devices with their start and end apart: 6 -> 12, of which waited for: 6 -> 12; matrix products, arithmetic and copies ran while one was open for 7% -> 7% of each run, Pallas kernels for 0% -> 0%
where the time goes in v1:
time: 1190 us; the launch traced here: 1180 us
  waiting for transfers between devices  638 us (54%)
  matrix products  279 us (23%)
  other arithmetic  113 us (9%)
  local copies, waits for them, and re-layouts  85.2 us (7%)
  blocking collectives  40.3 us (3%)
  between operations  17.2 us (1%)
    psum x1, waiting for transfers between devices, body(): lax.psum((grad_w_in, grad_b_in, grad_w_time, grad_gain1, grad_shift1, gra...  171 us
    psum x1, waiting for transfers between devices, body(): resid = hidden + lax.psum(attn_part, 'mp')  117 us
    psum x1, waiting for transfers between devices, body(): grad_act_two = lax.psum(grad_two_part, 'mp')  106 us
    psum x1, waiting for transfers between devices, body(): lax.psum(down_part.astype(jnp.bfloat16), 'mp').astype(jnp.float32)  100 us
    reduce_scatter x1, waiting for transfers between devices, body(): lax.psum_scatter(direct + norm_coeff * unit_rows, 'dp', scatter_dimension...  91.4 us
    dot_general x32, matrix products, probs_for(): jnp.einsum('qhd,khd->hqk', grad_blk, value_blk, preferred_element_type=jn...  59.4 us
    ppermute x7, waiting for transfers between devices, body(): lax.ppermute(value, 'dp', [(d, (d + 1) % ways) for d in range(ways)])  52.7 us
    dot_general x16, matrix products, value_step(): jnp.einsum('hqk,khd->qhd', weights_bf, block_rows(values_all, k_index, bl...  45.2 us
  transfers between devices with their start and end apart: 12, of which 12 were waited for; matrix products, arithmetic and copies ran while one was open for 7% of the time, Pallas kernels for 0%

profile of v1, /device:TPU:0, one launch (start us, length us, event | category | flops | bytes accessed | tf_op | source)
XLA Modules:
  0.0 1182.1 jit_solution(16861523187024260218)
XLA Ops:
  10.3 9.6 collective-permute-done
  20.6 9.5 collective-permute-done.1
  41.3 7.2 collective-permute-done.3
  82.3 10.7 gather_fusion
  106.7 98.0 %while.123 = (s32[]{:T(128)}, bf16[4,512,3,64]{1,3,2,0:T(8,128)(2,1)}, f32[4,3,512]{2,1,0:T(4,128)}, f32[4,3,512]{2,1,0:T(4,128)}, s32[4]{0:T(128)S(1)}, /*index...) while((s32[]{:T(128)}, ...), condition=%wide.region_11.12_spmd, body=%wide.region_4.11_spmd.sunk | while | flops 312155648 | bytes 10699101 | solution.py:101
  109.0 7.4 while.127
  117.0 12.5 %while.128 = (s32[]{:T(128)}, f32[512,3,64]{0,2,1:T(8,128)}, bf16[2048,3,64]{0,2,1:T(8,128)(2,1)S(1)}, s32[512]{0:T(512)S(1)}, s32[2048]{0:T(1024)S(1)}, /*index...) while((s32[]{:T(128)}, f32[512,3,64]{0,2,1:T(8,128)}, ...), condition=%wide.region_10.10_spmd.clone, body=%wide.region_9.9_spmd.clone.sunk | while | flops 205717504 | bytes 1926848 | solution.py:96
  133.5 7.4 while.127
  141.5 12.5 %while.128 = (s32[]{:T(128)}, f32[512,3,64]{0,2,1:T(8,128)}, bf16[2048,3,64]{0,2,1:T(8,128)(2,1)S(1)}, s32[512]{0:T(512)S(1)}, s32[2048]{0:T(1024)S(1)}, /*index...) while((s32[]{:T(128)}, f32[512,3,64]{0,2,1:T(8,128)}, ...), condition=%wide.region_10.10_spmd.clone, body=%wide.region_9.9_spmd.clone.sunk | while | flops 205717504 | bytes 1926848 | solution.py:96
  158.0 7.4 while.127
  166.0 12.5 %while.128 = (s32[]{:T(128)}, f32[512,3,64]{0,2,1:T(8,128)}, bf16[2048,3,64]{0,2,1:T(8,128)(2,1)S(1)}, s32[512]{0:T(512)S(1)}, s32[2048]{0:T(1024)S(1)}, /*index...) while((s32[]{:T(128)}, f32[512,3,64]{0,2,1:T(8,128)}, ...), condition=%wide.region_10.10_spmd.clone, body=%wide.region_9.9_spmd.clone.sunk | while | flops 205717504 | bytes 1926848 | solution.py:96
  182.5 7.4 while.127
  190.5 12.5 %while.128 = (s32[]{:T(128)}, f32[512,3,64]{0,2,1:T(8,128)}, bf16[2048,3,64]{0,2,1:T(8,128)(2,1)S(1)}, s32[512]{0:T(512)S(1)}, s32[2048]{0:T(1024)S(1)}, /*index...) while((s32[]{:T(128)}, f32[512,3,64]{0,2,1:T(8,128)}, ...), condition=%wide.region_10.10_spmd.clone, body=%wide.region_9.9_spmd.clone.sunk | while | flops 205717504 | bytes 1926848 | solution.py:96
  211.8 116.6 %all-reduce.8.cloned.1.call-done = f32[2048,768]{0,1:T(8,128)} async-done(((f32[2048,768]{0,1:T(8,128)}), f32[2048,768]{0,1:T(8,128)}) %all-reduce.8.cloned.1.call-update) | async-done | bytes 6291472 | tf_op jit(solution)/shard_map/psum | solution.py:244
  337.5 18.8 %multiply_convert_fusion = (bf16[2048,768]{1,0:T(8,128)(2,1)}, f32[2048,768]{1,0:T(8,128)}, f32[2048,768]{1,0:T(8,128)}) fusion(f32[768]{0:T(1024)S(1)} %copy-done.68, bf16[2048,768]{0,1:T(8,128)(2,1)S(1)} %add_convert_fusion.2, bf16[768,768]{1,0:T(8,128)(2,1)S(1)} %copy-done), kind=kOutput, calls=%fused_computation.93 | convolution fusion | flops 2519728128 | bytes 20057088 | tf_op jit(solution)/shard_map/dot_general | solution.py:247
  356.4 8.1 convert_reduce_fusion.1
  384.9 105.9 %all-reduce.10.cloned.1.call-done = f32[2048,768]{0,1:T(8,128)} async-done(((f32[2048,768]{0,1:T(8,128)}), f32[2048,768]{0,1:T(8,128)}) %all-reduce.10.cloned.1.call-update) | async-done | bytes 6291472 | tf_op jit(solution)/shard_map/psum | solution.py:263
  507.6 161.5 %while.126 = (s32[]{:T(128)}, bf16[2048,3,64]{0,2,1:T(8,128)(2,1)}, f32[2048,3,64]{0,2,1:T(8,128)}, f32[2048,3,64]{0,2,1:T(8,128)S(1)}, bf16[2048,3,64]{0,2,1:T(...) while((s32[]{:T(128)}, bf16[2048,3,64]{0,2,1:T(8,128)(2,1)}, ...), condition=%wide.region_25.26_spmd, body=%wide.region_19.25_spmd.sunk | while | flops 716768768 | bytes 27696096 | solution.py:185
  509.4 12.6 %while.129 = (s32[]{:T(128)}, f32[3,512]{1,0:T(4,128)S(1)}, bf16[2048,3,64]{0,2,1:T(8,128)(2,1)}, bf16[512,3,64]{0,2,1:T(8,128)(2,1)S(1)}, s32[512]{0:T(512)S(1)...) while((s32[]{:T(128)}, f32[3,512]{1,0:T(4,128)S(1)}, ...), condition=%wide.region_22.22_spmd.clone, body=%wide.region_20.21_spmd.clone.sunk | while | flops 206308864 | bytes 7647441 | solution.py:134
  522.0 25.2 %while.130 = (s32[]{:T(128)}, f32[512,3,64]{0,2,1:T(8,128)S(1)}, f32[2048,3,64]{0,2,1:T(8,128)}, f32[2048,3,64]{0,2,1:T(8,128)S(1)}, bf16[2048,3,64]{0,2,1:T(8,1...) while((s32[]{:T(128)}, f32[512,3,64]{0,2,1:T(8,128)S(1)}, ...), condition=%wide.region_24.24_spmd.clone, body=%wide.region_23.23_spmd.clone.sunk | while | flops 510459904 | bytes 18446580 | solution.py:180
  549.8 12.6 %while.129 = (s32[]{:T(128)}, f32[3,512]{1,0:T(4,128)S(1)}, bf16[2048,3,64]{0,2,1:T(8,128)(2,1)}, bf16[512,3,64]{0,2,1:T(8,128)(2,1)S(1)}, s32[512]{0:T(512)S(1)...) while((s32[]{:T(128)}, f32[3,512]{1,0:T(4,128)S(1)}, ...), condition=%wide.region_22.22_spmd.clone, body=%wide.region_20.21_spmd.clone.sunk | while | flops 206308864 | bytes 7647441 | solution.py:134
  562.3 25.2 %while.130 = (s32[]{:T(128)}, f32[512,3,64]{0,2,1:T(8,128)S(1)}, f32[2048,3,64]{0,2,1:T(8,128)}, f32[2048,3,64]{0,2,1:T(8,128)S(1)}, bf16[2048,3,64]{0,2,1:T(8,1...) while((s32[]{:T(128)}, f32[512,3,64]{0,2,1:T(8,128)S(1)}, ...), condition=%wide.region_24.24_spmd.clone, body=%wide.region_23.23_spmd.clone.sunk | while | flops 510459904 | bytes 18446580 | solution.py:180
  590.1 12.6 %while.129 = (s32[]{:T(128)}, f32[3,512]{1,0:T(4,128)S(1)}, bf16[2048,3,64]{0,2,1:T(8,128)(2,1)}, bf16[512,3,64]{0,2,1:T(8,128)(2,1)S(1)}, s32[512]{0:T(512)S(1)...) while((s32[]{:T(128)}, f32[3,512]{1,0:T(4,128)S(1)}, ...), condition=%wide.region_22.22_spmd.clone, body=%wide.region_20.21_spmd.clone.sunk | while | flops 206308864 | bytes 7647441 | solution.py:134
  602.7 25.2 %while.130 = (s32[]{:T(128)}, f32[512,3,64]{0,2,1:T(8,128)S(1)}, f32[2048,3,64]{0,2,1:T(8,128)}, f32[2048,3,64]{0,2,1:T(8,128)S(1)}, bf16[2048,3,64]{0,2,1:T(8,1...) while((s32[]{:T(128)}, f32[512,3,64]{0,2,1:T(8,128)S(1)}, ...), condition=%wide.region_24.24_spmd.clone, body=%wide.region_23.23_spmd.clone.sunk | while | flops 510459904 | bytes 18446580 | solution.py:180
  630.5 12.5 %while.129 = (s32[]{:T(128)}, f32[3,512]{1,0:T(4,128)S(1)}, bf16[2048,3,64]{0,2,1:T(8,128)(2,1)}, bf16[512,3,64]{0,2,1:T(8,128)(2,1)S(1)}, s32[512]{0:T(512)S(1)...) while((s32[]{:T(128)}, f32[3,512]{1,0:T(4,128)S(1)}, ...), condition=%wide.region_22.22_spmd.clone, body=%wide.region_20.21_spmd.clone.sunk | while | flops 206308864 | bytes 7647441 | solution.py:134
  643.0 25.2 %while.130 = (s32[]{:T(128)}, f32[512,3,64]{0,2,1:T(8,128)S(1)}, f32[2048,3,64]{0,2,1:T(8,128)}, f32[2048,3,64]{0,2,1:T(8,128)S(1)}, bf16[2048,3,64]{0,2,1:T(8,1...) while((s32[]{:T(128)}, f32[512,3,64]{0,2,1:T(8,128)S(1)}, ...), condition=%wide.region_24.24_spmd.clone, body=%wide.region_23.23_spmd.clone.sunk | while | flops 510459904 | bytes 18446580 | solution.py:180
  695.7 100.5 %all-reduce.14.cloned.1.call-done = (bf16[2048,768]{0,1:T(8,128)(2,1)}, bf16[2048,768]{0,1:T(8,128)(2,1)}) async-done(((bf16[2048,768]{0,1:T(8,128)(2,1)}, bf16[2048,768]{0,1:T(8,128)(2,1)}), (bf16[2048,768]{0,1:T(8,128)(2,1)}, bf16[2048,768]{0,1:T(8,128)(2,1)})) %all-reduce.14.cloned.1.call-update) | async-done | bytes 6291472 | tf_op jit(solution)/shard_map/psum | solution.py:251
  825.2 13.1 %scatter_custom_fusion = f32[8193,128]{1,0:T(8,128)} fusion(s32[2048]{0:T(1024)} %get-tuple-element.1347, f32[]{:T(128)} %constant.392.clone.1, f32[2048,128]{1,0:T(8,128)} %get-tuple-element.1355, f32[]{:T(128)S(6)} %div.136), kind=kCustom, calls=%fused_computation.122 | custom fusion | flops 524288 | bytes 5243908 | tf_op jit(solution)/shard_map/scatter-add | solution.py:297
  848.3 7.2 add_add_fusion.3
  862.2 40.3 %all-reduce = (f32[768]{0:T(1024)}, f32[768]{0:T(1024)}, f32[768]{0:T(1024)}, f32[768]{0:T(1024)}, f32[768]{0:T(1024)}, /*index=5*/f32[768]{0:T(1024)}, f32[768]{0:T(1024)}) all-reduce(f32[768]{0:T(1024)S(1)} %get-tuple-element.1324, f32[768]{0:T(1024)S(1)} %get-tuple-element.1186, ...), channel_id=1, replica_groups=mesh['dp'=8,'mp'=4] {'dp'}, use_global_device_ids=true, to_apply=%region_34.35 | all-reduce | flops 5376 | bytes 43008 | tf_op jit(solution)/shard_map/psum | solution.py:302
  902.5 171.4 %all-reduce.12.cloned.1.call-done = (f32[128,768]{1,0:T(8,128)}, f32[128,768]{1,0:T(8,128)}, f32[3,768,192]{1,2,0:T(8,128)}, f32[192,768]{1,0:T(8,128)}, f32[768,768]{1,0:T(8,128)}, /*index=5*/f32[768,768]{1,0:T(8,128)}) async-done(((f32[128,768]{1,0:T(8,128)}, f32[128,768]{1,0:T(8,128)}, f32[3,768,192]{1,2,0:T(8,128)}, f32[192,768]{1,0:T(8,128)}, f32[768,768]{1,0:T(8,128)}, ...) | async-done | bytes 7864336 | tf_op jit(solution)/shard_map/psum | solution.py:302
  1073.8 91.4 %reduce-scatter.2.cloned.1.call-done = f32[1024,128]{1,0:T(8,128)} async-done(((f32[8192,128]{1,0:T(8,128)}), f32[1024,128]{1,0:T(8,128)}) %reduce-scatter.2.cloned.1.call-update) | async-done | bytes 524304 | tf_op jit(solution)/shard_map/reduce_scatter | solution.py:298
  (665 shorter events, 449.7 us)
Async XLA Ops:
  7.2 330.3 %copy-start = (bf16[768,768]{1,0:T(8,128)(2,1)S(1)}, bf16[768,768]{1,0:T(8,128)(2,1)}, u32[]{:S(2)}) copy-start(bf16[768,768]{1,0:T(8,128)(2,1)} %param.45) | copy-start | bytes 3538948
  7.2 321.2 %all-reduce.8.cloned.1.call-start = ((), (), s32[]{:S(2)}) async-start(), calls=%async_computation.1 | async-start | bytes 12582912 | tf_op jit(solution)/shard_map/psum | solution.py:244
  7.2 12.6 %collective-permute-start = (bf16[1024,128]{1,0:T(8,128)(2,1)}, bf16[1024,128]{1,0:T(8,128)(2,1)S(1)}, u32[]{:S(2)}, u32[]{:S(2)}) collective-permute-start(bf16[1024,128]{1,0:T(8,128)(2,1)} %param.35), channel_id=1, source_target_pairs={{0,4},{4,8},{8,12},{12,16},{16,20},{20,24},{24,28},{28,0},{1,5},{5... | collective-permute-start | bytes 786440 | tf_op jit(solution)/shard_map/ppermute | solution.py:214
  19.8 10.2 copy-start.40
  19.8 10.2 collective-permute-start.1
  30.0 9.3 collective-permute-start.2
  33.4 65.5 %copy-start.23 = (bf16[2048,64]{0,1:T(8,128)(2,1)}, bf16[2048,64]{0,1:T(8,128)(2,1)S(1)}, u32[]{:S(2)}) copy-start(bf16[2048,64]{0,1:T(8,128)(2,1)S(1)} %get-tuple-element.1345) | copy-start | bytes 786436
  39.3 9.2 collective-permute-start.3
  40.0 52.9 %copy-start.55 = (pred[2048]{0:T(1024)(128)(4,1)}, pred[2048]{0:T(1024)(128)(4,1)S(1)}, u32[]{:S(2)}) copy-start(pred[2048]{0:T(1024)(128)(4,1)S(1)} %compare_and_fusion) | copy-start | bytes 6148
  48.5 9.4 collective-permute-start.4
  51.3 41.7 %copy-start.43 = (f32[2048]{0:T(1024)}, f32[2048]{0:T(1024)S(1)}, u32[]{:S(2)}) copy-start(f32[2048]{0:T(1024)S(1)} %get-tuple-element.1349) | copy-start | bytes 24580
  57.9 9.9 collective-permute-start.5
  67.8 9.1 collective-permute-start.6
  76.9 16.1 %copy-start.7 = (bf16[8192,128]{1,0:T(8,128)(2,1)}, bf16[8192,128]{1,0:T(8,128)(2,1)S(1)}, u32[]{:S(2)}) copy-start(bf16[8192,128]{1,0:T(8,128)(2,1)S(1)} %constant_dynamic-update-slice_fusion.1) | copy-start | bytes 6291460
  106.7 101.1 %copy-start.29 = (bf16[192,768]{1,0:T(8,128)(2,1)S(1)}, bf16[192,768]{1,0:T(8,128)(2,1)}, u32[]{:S(2)}) copy-start(bf16[192,768]{1,0:T(8,128)(2,1)} %param.42) | copy-start | bytes 884740
  211.6 279.1 %all-reduce.10.cloned.1.call-start = ((), (), s32[]{:S(2)}) async-start(), calls=%async_computation.2 | async-start | bytes 12582912 | tf_op jit(solution)/shard_map/psum | solution.py:263
  335.4 20.9 %slice-start.2 = ((s8[6291456]{0:T(1024)(128)(4,1)}), s8[4194304]{0:T(1024)(128)(4,1)S(1)}, s32[]{:S(2)}) async-start(s8[6291456]{0:T(1024)(128)(4,1)} %bitcast.204), calls=%async_computation.8 | async-start | bytes 8388608
  337.5 18.9 %copy-start.21 = (bf16[2048,768]{0,1:T(8,128)(2,1)}, bf16[2048,768]{0,1:T(8,128)(2,1)S(1)}, u32[]{:S(2)}) copy-start(bf16[2048,768]{0,1:T(8,128)(2,1)S(1)} %add_convert_fusion.2) | copy-start | bytes 9437188
  337.5 18.9 %slice-start.3 = ((s8[6291456]{0:T(1024)(128)(4,1)}), s8[2097152]{0:T(1024)(128)(4,1)S(1)}, s32[]{:S(2)}) async-start(s8[6291456]{0:T(1024)(128)(4,1)} %bitcast.204), calls=%async_computation.9 | async-start | bytes 4194304
  337.5 18.9 %copy-start.65 = (bf16[768,768]{1,0:T(8,128)(2,1)S(1)}, bf16[768,768]{1,0:T(8,128)(2,1)}, u32[]{:S(2)}) copy-start(bf16[768,768]{1,0:T(8,128)(2,1)} %param.47) | copy-start | bytes 3538948
  370.8 425.4 %all-reduce.14.cloned.1.call-start = ((), (), s32[]{:S(2)}) async-start(), calls=%async_computation.5 | async-start | bytes 12582912 | tf_op jit(solution)/shard_map/psum | solution.py:251
  490.7 10.6 slice-start.4
  676.2 397.6 %all-reduce.12.cloned.1.call-start = ((), (), s32[]{:S(2)}) async-start(), calls=%async_computation.4 | async-start | bytes 15728640 | tf_op jit(solution)/shard_map/psum | solution.py:302
  692.4 103.8 %copy-start.39 = (f32[2048]{0:T(1024)S(1)}, f32[2048]{0:T(1024)}, u32[]{:S(2)}) copy-start(f32[2048]{0:T(1024)} %copy-done.38) | copy-start | bytes 24580
  692.4 103.7 %copy-start.54 = (f32[768]{0:T(1024)S(1)}, f32[768]{0:T(1024)}, u32[]{:S(2)}) copy-start(f32[768]{0:T(1024)} %param.39) | copy-start | bytes 9220
  692.4 115.4 %slice-start.6 = ((s8[6291456]{0:T(1024)(128)(4,1)}), s8[2097152]{0:T(1024)(128)(4,1)S(1)}, s32[]{:S(2)}) async-start(s8[6291456]{0:T(1024)(128)(4,1)} %bitcast.208), calls=%async_computation.12 | async-start | bytes 4194304
  796.2 11.6 slice-start
  796.2 11.6 slice-start.7
  817.6 347.6 %reduce-scatter.2.cloned.1.call-start = ((), (), s32[]{:S(2)}) async-start(), calls=%async_computation.3 | async-start | bytes 4718592 | tf_op jit(solution)/shard_map/reduce_scatter | solution.py:298
  823.7 14.6 %copy-start.8 = (bf16[8192,128]{1,0:T(8,128)(2,1)S(1)}, bf16[8192,128]{1,0:T(8,128)(2,1)}, u32[]{:S(2)}) copy-start(bf16[8192,128]{1,0:T(8,128)(2,1)} %copy-done.7) | copy-start | bytes 6291460
  823.7 14.6 %copy-start.46 = (f32[8192]{0:T(1024)S(1)}, f32[8192]{0:T(1024)}, u32[]{:S(2)}) copy-start(f32[8192]{0:T(1024)} %get-tuple-element.1343) | copy-start | bytes 98308
  1073.8 98.7 %copy-start.28 = (f32[768,768]{1,0:T(8,128)S(1)}, f32[768,768]{1,0:T(8,128)}, u32[]{:S(2)}) copy-start(f32[768,768]{1,0:T(8,128)} %get-tuple-element.2136) | copy-start | bytes 7077892
  (58 other events, 228.9 us)
Sparse Core Ops, SparseCore 0:
  211.7 116.6 all-reduce.7
  370.9 119.7 all-reduce.9
  676.3 119.7 all-reduce.13
  817.7 256.0 all-reduce.11
  1077.9 87.2 reduce-scatter.1
